TPU v7x, 256 devices: a whole 4x4x8 slice. The times are simulated.
256 devices in a mesh: fsdp: 32 (over y, x, core), rep: 8 (over z).
Axes of the slice: x: 4, y: 4, z: 8, core: 2. Of those that a mesh axis runs over, the one named last changes fastest.
Arguments:
- tokens: bfloat16 [8, 4096, 2048], P('rep', 'fsdp'), may hold values from -6 to 6
- upstream: bfloat16 [8, 7168, 4096], P('rep', 'fsdp'), may hold values from -0.25 to 0.25
- weight: bfloat16 [2, 7168, 2048], P(None, 'fsdp'), may hold values from -0.125 to 0.125
- feedback: float32 [8, 2, 7168, 2048], P('rep', None, 'fsdp'), may hold values from -6 to 6
- momentum: float32 [2, 7168, 2048], P(None, 'fsdp', 'rep'), may hold values from -6 to 6
- right_factor: float32 [2, 7168, 64], P(None, 'fsdp'), may hold values from -6 to 6
Outputs:
- feedback_next: float32 [8, 2, 7168, 2048], P('rep', None, 'fsdp')
- momentum_next: float32 [2, 7168, 2048], P(None, 'fsdp', 'rep')
- weight_next: bfloat16 [2, 7168, 2048], P(None, 'fsdp', 'rep')
- right_next: float32 [2, 7168, 64], P(None, 'fsdp')
All inputs are finite; a program needn't handle non-finite values.
Results may differ from a plain program's by a relative error of at most 0.0023.
Values may be sent and summed in bfloat16 or wider, within the bound.
A program may use at most 128 MiB of HBM per device.

v0:
```python
import jax
import jax.numpy as jnp
from jax import lax
from jax.sharding import PartitionSpec as P

momentum_decay = 0.9
step_rate = 0.05
highest = lax.Precision.HIGHEST


def silu_pair(gate_pre):
    sigmoid = jax.nn.sigmoid(gate_pre)
    return (gate_pre * sigmoid, sigmoid * (1.0 + gate_pre * (1.0 - sigmoid)))


def solve_basis(factor, gram_matrix):
    lower_factor = jnp.linalg.cholesky(gram_matrix)
    return lax.linalg.triangular_solve(
        lower_factor, factor, left_side=False, lower=True, transpose_a=True
    )


def local_gram(factor):
    return jnp.einsum("kdr,kds->krs", factor, factor, precision=highest)


def per_device(tokens, upstream, weight, feedback, momentum, right_factor):
    own_rows = tokens[0]
    cotangents = upstream[0]
    contract_last = (((1,), (1,)), ((), ()))
    segment = lax.all_gather(own_rows, "fsdp", axis=0, tiled=True)
    cotangent_wide = cotangents.astype(jnp.float32)
    gate_pre = lax.dot_general(
        weight[0], segment, contract_last, preferred_element_type=jnp.float32
    )
    up_pre = lax.dot_general(weight[1], segment, contract_last, preferred_element_type=jnp.float32)
    activated, derivative = silu_pair(gate_pre)
    grad_gate = (cotangent_wide * up_pre * derivative).astype(jnp.bfloat16)
    grad_up = (cotangent_wide * activated).astype(jnp.bfloat16)
    term_gate = jnp.dot(grad_gate, segment, preferred_element_type=jnp.float32)
    term_up = jnp.dot(grad_up, segment, preferred_element_type=jnp.float32)
    gradient = jnp.stack([term_gate, term_up])
    delta = gradient + feedback[0]
    left_part = jnp.einsum("kfd,kfr->kdr", delta, right_factor, precision=highest)
    replicas = lax.axis_size("rep")
    left_mean = lax.psum(left_part, ("fsdp", "rep")) / replicas
    basis = solve_basis(left_mean, local_gram(left_mean))
    right_part = jnp.einsum("kfd,kdr->kfr", delta, basis, precision=highest)
    right_next = lax.psum(right_part, "rep") / replicas
    approx = jnp.einsum("kdr,kfr->kfd", basis, right_next, precision=highest)
    feedback_next = (delta - approx)[None]
    slab_cols = momentum.shape[2]
    slab_start = lax.axis_index("rep") * slab_cols
    approx_slab = lax.dynamic_slice_in_dim(approx, slab_start, slab_cols, 2)
    weight_slab = lax.dynamic_slice_in_dim(weight, slab_start, slab_cols, 2)
    momentum_next = momentum_decay * momentum + approx_slab
    weight_next = (weight_slab.astype(jnp.float32) - step_rate * momentum_next).astype(jnp.bfloat16)
    return (feedback_next, momentum_next, weight_next, right_next)


def solution(mesh):
    placed = (
        P("rep", "fsdp", None),
        P("rep", "fsdp", None),
        P(None, "fsdp", None),
        P("rep", None, "fsdp", None),
        P(None, "fsdp", "rep"),
        P(None, "fsdp", None),
    )
    return jax.shard_map(
        per_device,
        mesh=mesh,
        in_specs=placed,
        out_specs=(
            P("rep", None, "fsdp", None),
            P(None, "fsdp", "rep"),
            P(None, "fsdp", "rep"),
            P(None, "fsdp", None),
        ),
        check_vma=False,
    )
```

profile of v0, /device:TPU:2, one launch (start us, length us, event | category | flops | bytes accessed | tf_op | source)
XLA Modules:
  0.0 520.9 jit_solution(15495969798062645339)
XLA Ops:
  7.2 0.0 copy-start
  7.2 0.0 all-gather.3.cloned.1.call-start
  7.2 0.7 all-gather.3.cloned.1.call-update
  7.9 0.0 all-reduce.3.cloned.1.call-start
  8.0 83.1 %all-gather.3.cloned.1.call-done = bf16[1,4096,2048]{2,1,0:T(8,128)(2,1)} async-done(((bf16[1,128,2048]{2,1,0:T(8,128)(2,1)}), bf16[1,4096,2048]{2,1,0:T(8,128)(2,1)}) %all-gather.3.cloned.1.call-update) | async-done | bytes 16777232 | tf_op jit(solution)/shard_map/all_gather | solution.py:31
  91.1 13.0 %fusion.4 = f32[224,4096]{1,0:T(8,128)} fusion(bf16[1,4096,2048]{2,1,0:T(8,128)(2,1)} %all-gather.3.cloned.1.call-done, bf16[2,224,2048]{2,1,0:T(8,128)(2,1)} %param.8), kind=kOutput, calls=%fused_computation.4 | convolution fusion | flops 3758096384 | bytes 21364736 | tf_op jit(solution)/shard_map/dot_general | solution.py:33
  104.1 20.5 %fusion.25 = f32[1,224,2048]{2,1,0:T(8,128)S(1)} fusion(bf16[1,4096,2048]{2,1,0:T(8,128)(2,1)} %all-gather.3.cloned.1.call-done, f32[224,4096]{1,0:T(8,128)} %fusion.4, bf16[1,224,4096]{2,1,0:T(8,128)(2,1)} %param.7, bf16[2,224,2048]{2,1,0:T(8,128)(2,1)} %param.8), kind=kOutput, calls=%fused_computation.21 | convolution fusion | flops 7526285312 | bytes 41811968 | tf_op jit(solution)/shard_map/dot_general | solution.py:40
  124.7 0.0 copy-start.1
  124.7 9.7 %fusion.30 = f32[1,224,2048]{2,1,0:T(8,128)S(1)} fusion(bf16[1,4096,2048]{2,1,0:T(8,128)(2,1)} %all-gather.3.cloned.1.call-done, f32[224,4096]{1,0:T(8,128)} %fusion.4, bf16[1,224,4096]{2,1,0:T(8,128)(2,1)} %param.7), kind=kOutput, calls=%fused_computation.22 | convolution fusion | flops 3764518912 | bytes 24117248 | tf_op jit(solution)/shard_map/dot_general | solution.py:41
  134.4 0.0 copy-start.3
  134.4 1.2 copy-done.3
  135.7 0.0 copy-done
  135.7 0.0 copy-done.1
  135.7 3.6 fusion.57
  139.3 0.0 all-reduce.3.cloned.1.call-update
  139.3 0.2 all-reduce.5.cloned.1.call-start
  139.6 258.4 %all-reduce.3.cloned.1.call-done = f32[2,2048,64]{1,2,0:T(8,128)} async-done(((f32[2,2048,64]{1,2,0:T(8,128)}), f32[2,2048,64]{1,2,0:T(8,128)}) %all-reduce.3.cloned.1.call-update) | async-done | bytes 1048592 | tf_op jit(solution)/shard_map/psum | solution.py:46
  397.9 2.7 fusion.40
  400.6 0.1 copy.12
  400.7 11.7 %custom-call.7 = f32[2,64,64]{2,1,0:T(8,128)S(1)} custom-call(f32[2,64,64]{2,1,0:T(8,128)S(1)} %fusion.51), custom_call_target="Cholesky" | custom-call | tf_op jit(solution)/shard_map/jit(cholesky)/cholesky | solution.py:17
  412.5 0.1 compare_reduce_fusion
  412.6 0.1 select_bitcast_fusion
  412.7 9.8 %custom-call.8 = f32[2,1,64,64]{2,3,1,0:T(8,128)S(1)} custom-call(f32[2,1,64,64]{3,2,1,0:T(8,128)S(1)} %select_bitcast_fusion), custom_call_target="InvertDiagBlocksLowerTriangular" | custom-call | tf_op jit(solution)/shard_map/triangular_solve | solution.py:18
  422.5 2.3 fusion.38
  424.9 7.1 %fusion.56 = f32[2,224,64]{1,2,0:T(8,128)} fusion(f32[2,2048,64]{1,2,0:T(8,128)S(1)} %fusion.38, f32[1,224,2048]{2,1,0:T(8,128)} %copy-done.3, f32[1,224,2048]{2,1,0:T(8,128)S(1)} %fusion.25, f32[1,2,224,2048]{3,2,1,0:T(8,128)} %param.9), kind=kOutput, calls=%fused_computation.52 | convolution fusion | flops 706478080 | bytes 8503296 | tf_op jit(solution)/shard_map/kfd,kdr->kfr/dot_general | solution.py:48
  432.0 0.0 all-reduce.5.cloned.1.call-update
  432.0 71.5 %all-reduce.5.cloned.1.call-done = f32[2,224,64]{1,2,0:T(8,128)} async-done(((f32[2,224,64]{1,2,0:T(8,128)}), f32[2,224,64]{1,2,0:T(8,128)}) %all-reduce.5.cloned.1.call-update) | async-done | bytes 114704 | tf_op jit(solution)/shard_map/psum | solution.py:49
  503.5 0.0 copy-start.2
  503.5 1.1 broadcast_multiply_fusion
  504.5 0.0 copy-start.4
  504.5 3.1 fusion.58
  507.6 0.0 copy-done.2
  507.6 0.0 copy-start.5
  507.6 4.8 subtract_bitcast_fusion
  512.5 0.0 copy-done.4
  512.5 0.0 copy-done.5
  512.5 1.9 subtract_convert_fusion
  (4 shorter events, 0.1 us)
Async XLA Ops:
  7.2 128.5 %copy-start = (f32[2,224,64]{1,2,0:T(8,128)S(1)}, f32[2,224,64]{1,2,0:T(8,128)}, u32[]{:S(2)}) copy-start(f32[2,224,64]{1,2,0:T(8,128)} %param.11) | copy-start | bytes 344068
  7.2 83.9 %all-gather.3.cloned.1.call-start = ((), (), s32[]{:S(2)}) async-start(), calls=%async_computation.2 | async-start | bytes 17301504 | tf_op jit(solution)/shard_map/all_gather | solution.py:31
  7.9 390.0 %all-reduce.3.cloned.1.call-start = ((), (), s32[]{:S(2)}) async-start(), calls=%async_computation | async-start | bytes 2097152 | tf_op jit(solution)/shard_map/psum | solution.py:46
  124.7 11.0 %copy-start.1 = (f32[1,2,224,2048]{3,2,1,0:T(8,128)S(1)}, f32[1,2,224,2048]{3,2,1,0:T(8,128)}, u32[]{:S(2)}) copy-start(f32[1,2,224,2048]{3,2,1,0:T(8,128)} %param.9) | copy-start | bytes 11010052
  134.4 1.3 copy-start.3
  139.3 364.2 %all-reduce.5.cloned.1.call-start = ((), (), s32[]{:S(2)}) async-start(), calls=%async_computation.1 | async-start | bytes 262144 | tf_op jit(solution)/shard_map/psum | solution.py:49
  503.5 4.2 copy-start.2
  504.5 8.0 %copy-start.4 = (f32[2,224,64]{1,2,0:T(8,128)}, f32[2,224,64]{1,2,0:T(8,128)S(1)}, u32[]{:S(2)}) copy-start(f32[2,224,64]{1,2,0:T(8,128)S(1)} %broadcast_multiply_fusion) | copy-start | bytes 344068
  507.6 4.9 copy-start.5
Sparse Core Ops, SparseCore 0:
  10.5 80.4 all-gather.2
  139.4 258.4 all-reduce.2
  432.1 71.3 all-reduce.4
where the time goes:
time: 521 us
  waiting for transfers between devices  414 us (79%)
  matrix products  62.1 us (12%)
  other arithmetic  29.6 us (6%)
  between operations  13.9 us (3%)
    psum x1, waiting for transfers between devices, per_device(): left_mean = lax.psum(left_part, ('fsdp', 'rep')) / replicas  258 us
    all_gather x1, waiting for transfers between devices, per_device(): segment = lax.all_gather(own_rows, 'fsdp', axis=0, tiled=True)  83.1 us
    psum x1, waiting for transfers between devices, per_device(): right_next = lax.psum(right_part, 'rep') / replicas  71.5 us
    dot_general x1, matrix products, per_device(): term_gate = jnp.dot(grad_gate, segment, preferred_element_type=jnp.float32)  20.5 us
    dot_general x1, matrix products, per_device(): lax.dot_general(weight[0], segment, contract_last, preferred_element_type...  13 us
    another operation x4, other arithmetic, solve_basis(): lower_factor = jnp.linalg.cholesky(gram_matrix)  11.9 us
  transfers between devices with their start and end apart: 3, of which 3 were waited for; matrix products, arithmetic and copies ran while one was open for 0% of the time, Pallas kernels for 0%

commit v1 on v0

--- a/solution.py
+++ b/solution.py
@@ -28,7 +28,9 @@
     own_rows = tokens[0]
     cotangents = upstream[0]
     contract_last = (((1,), (1,)), ((), ()))
-    segment = lax.all_gather(own_rows, "fsdp", axis=0, tiled=True)
+    segment = jnp.concatenate(
+        lax.all_to_all(jnp.stack([own_rows] * lax.axis_size("fsdp")), "fsdp", 0, 0), axis=0
+    )
     cotangent_wide = cotangents.astype(jnp.float32)
     gate_pre = lax.dot_general(
         weight[0], segment, contract_last, preferred_element_type=jnp.float32

time: 521 us -> 631 us (1.21)
  blocking collectives: 0 us -> 192 us
  waiting for transfers between devices: 414 us -> 331 us
    all_to_all x0 -> x1, blocking collectives: none -> 192 us  [per_device(): lax.all_to_all(jnp.stack([own_rows] * lax.axis_size('fsdp')), 'fsdp', 0, 0)]
    all_gather x1 -> x0, waiting for transfers between devices: 83.1 us -> none  [per_device(): segment = lax.all_gather(own_rows, 'fsdp', axis=0, tiled=True)]
  transfers between devices with their start and end apart: 3 -> 2, of which waited for: 3 -> 2; matrix products, arithmetic and copies ran while one was open for 0% -> 0% of each run, Pallas kernels for 0% -> 0%
where the time goes in v1:
time: 631 us
  waiting for transfers between devices  331 us (52%)
  blocking collectives  192 us (30%)
  matrix products  59.2 us (9%)
  other arithmetic  29.6 us (5%)
  between operations  14.2 us (2%)
    psum x1, waiting for transfers between devices, per_device(): left_mean = lax.psum(left_part, ('fsdp', 'rep')) / replicas  259 us
    all_to_all x1, blocking collectives, per_device(): lax.all_to_all(jnp.stack([own_rows] * lax.axis_size('fsdp')), 'fsdp', 0, 0)  192 us
    psum x1, waiting for transfers between devices, per_device(): right_next = lax.psum(right_part, 'rep') / replicas  71.5 us
    dot_general x1, matrix products, per_device(): term_gate = jnp.dot(grad_gate, segment, preferred_element_type=jnp.float32)  20.2 us
  transfers between devices with their start and end apart: 2, of which 2 were waited for; matrix products, arithmetic and copies ran while one was open for 0% of the time, Pallas kernels for 0%

profile of v1, /device:TPU:2, one launch (start us, length us, event | category | flops | bytes accessed | tf_op | source)
XLA Modules:
  0.0 631.0 jit_solution(16134316759440331017)
XLA Ops:
  7.2 0.0 copy-start
  7.2 0.0 all-reduce.3.cloned.1.call-start
  7.2 3.6 stack.12
  10.8 0.0 copy-start.6
  10.9 192.2 %all_to_all.5 = bf16[32,128,2048]{2,1,0:T(8,128)(2,1)} all-to-all(bf16[32,128,2048]{2,1,0:T(8,128)(2,1)S(1)} %stack.12), channel_id=1, replica_groups=mesh['fsdp'=32,'rep'=8] {'fsdp'}, dimensions={0} | all-to-all | bytes 33554432 | tf_op jit(solution)/shard_map/all_to_all | solution.py:32
  203.0 0.0 copy-done.6
  203.0 10.6 %fusion.10 = f32[224,4096]{1,0:T(8,128)} fusion(bf16[4096,2048]{1,0:T(8,128)(2,1)} %bitcast.48, bf16[2,224,2048]{2,1,0:T(8,128)(2,1)S(1)} %copy-done.6), kind=kOutput, calls=%fused_computation.16 | convolution fusion | flops 3758096384 | bytes 21364736 | tf_op jit(solution)/shard_map/dot_general | solution.py:35
  213.6 20.2 %convolution_bitcast_fusion.1 = f32[1,224,2048]{2,1,0:T(8,128)S(1)} fusion(bf16[4096,2048]{1,0:T(8,128)(2,1)} %bitcast.49, f32[224,4096]{1,0:T(8,128)} %fusion.10, bf16[1,224,4096]{2,1,0:T(8,128)(2,1)} %param.7, bf16[2,224,2048]{2,1,0:T(8,128)(2,1)} %param.8), kind=kOutput, calls=%fused_computation.9 | convolution fusion | flops 7526285312 | bytes 41811968 | tf_op jit(solution)/shard_map/dot_general | solution.py:42
  233.8 0.0 copy-start.1
  233.8 9.7 %convolution_bitcast_fusion = f32[1,224,2048]{2,1,0:T(8,128)S(1)} fusion(bf16[4096,2048]{1,0:T(8,128)(2,1)} %bitcast.50, f32[224,4096]{1,0:T(8,128)} %fusion.10, bf16[1,224,4096]{2,1,0:T(8,128)(2,1)} %param.7), kind=kOutput, calls=%fused_computation.8 | convolution fusion | flops 3764518912 | bytes 24117248 | tf_op jit(solution)/shard_map/dot_general | solution.py:43
  243.5 0.0 copy-start.3
  243.5 1.2 copy-done.3
  244.8 0.0 copy-done
  244.8 0.0 copy-done.1
  244.8 3.6 fusion.26
  248.4 0.0 all-reduce.3.cloned.1.call-update
  248.4 0.2 all-reduce.5.cloned.1.call-start
  248.7 259.0 %all-reduce.3.cloned.1.call-done = f32[2,2048,64]{1,2,0:T(8,128)} async-done(((f32[2,2048,64]{1,2,0:T(8,128)}), f32[2,2048,64]{1,2,0:T(8,128)}) %all-reduce.3.cloned.1.call-update) | async-done | bytes 1048592 | tf_op jit(solution)/shard_map/psum | solution.py:48
  507.7 2.7 fusion.8
  510.4 0.1 copy.12
  510.5 11.7 %custom-call.7 = f32[2,64,64]{2,1,0:T(8,128)S(1)} custom-call(f32[2,64,64]{2,1,0:T(8,128)S(1)} %fusion.20), custom_call_target="Cholesky" | custom-call | tf_op jit(solution)/shard_map/jit(cholesky)/cholesky | solution.py:17
  522.3 0.1 compare_reduce_fusion
  522.4 0.1 select_bitcast_fusion
  522.5 9.8 %custom-call.8 = f32[2,1,64,64]{2,3,1,0:T(8,128)S(1)} custom-call(f32[2,1,64,64]{3,2,1,0:T(8,128)S(1)} %select_bitcast_fusion), custom_call_target="InvertDiagBlocksLowerTriangular" | custom-call | tf_op jit(solution)/shard_map/triangular_solve | solution.py:18
  532.3 2.3 fusion.6
  534.6 7.1 %fusion.25 = f32[2,224,64]{1,2,0:T(8,128)} fusion(f32[2,2048,64]{1,2,0:T(8,128)S(1)} %fusion.6, f32[1,224,2048]{2,1,0:T(8,128)} %copy-done.3, f32[1,224,2048]{2,1,0:T(8,128)S(1)} %convolution_bitcast_fusion.1, f32[1,2,224,2048]{3,2,1,0:T(8,128)} %param.9), kind=kOutput, calls=%fused_computation.38 | convolution fusion | flops 706478080 | bytes 8503296 | tf_op jit(solution)/shard_map/kfd,kdr->kfr/dot_general | solution.py:50
  541.7 0.0 all-reduce.5.cloned.1.call-update
  541.8 71.5 %all-reduce.5.cloned.1.call-done = f32[2,224,64]{1,2,0:T(8,128)} async-done(((f32[2,224,64]{1,2,0:T(8,128)}), f32[2,224,64]{1,2,0:T(8,128)}) %all-reduce.5.cloned.1.call-update) | async-done | bytes 114704 | tf_op jit(solution)/shard_map/psum | solution.py:51
  613.2 0.0 copy-start.2
  613.2 1.1 broadcast_multiply_fusion
  614.3 0.0 copy-start.4
  614.3 3.1 fusion.27
  617.4 0.0 copy-done.2
  617.4 0.0 copy-start.5
  617.4 4.8 subtract_bitcast_fusion
  622.2 0.0 copy-done.4
  622.2 0.0 copy-done.5
  622.2 1.9 subtract_convert_fusion
  (4 shorter events, 0.1 us)
Async XLA Ops:
  7.2 237.6 %copy-start = (f32[2,224,64]{1,2,0:T(8,128)S(1)}, f32[2,224,64]{1,2,0:T(8,128)}, u32[]{:S(2)}) copy-start(f32[2,224,64]{1,2,0:T(8,128)} %param.11) | copy-start | bytes 344068
  7.2 500.5 %all-reduce.3.cloned.1.call-start = ((), (), s32[]{:S(2)}) async-start(), calls=%async_computation.1 | async-start | bytes 2097152 | tf_op jit(solution)/shard_map/psum | solution.py:48
  10.8 192.2 %copy-start.6 = (bf16[2,224,2048]{2,1,0:T(8,128)(2,1)S(1)}, bf16[2,224,2048]{2,1,0:T(8,128)(2,1)}, u32[]{:S(2)}) copy-start(bf16[2,224,2048]{2,1,0:T(8,128)(2,1)} %param.8) | copy-start | bytes 5505028
  233.8 11.0 %copy-start.1 = (f32[1,2,224,2048]{3,2,1,0:T(8,128)S(1)}, f32[1,2,224,2048]{3,2,1,0:T(8,128)}, u32[]{:S(2)}) copy-start(f32[1,2,224,2048]{3,2,1,0:T(8,128)} %param.9) | copy-start | bytes 11010052
  243.5 1.3 copy-start.3
  248.4 364.8 %all-reduce.5.cloned.1.call-start = ((), (), s32[]{:S(2)}) async-start(), calls=%async_computation.2 | async-start | bytes 262144 | tf_op jit(solution)/shard_map/psum | solution.py:51
  613.2 4.2 copy-start.2
  614.3 8.0 %copy-start.4 = (f32[2,224,64]{1,2,0:T(8,128)}, f32[2,224,64]{1,2,0:T(8,128)S(1)}, u32[]{:S(2)}) copy-start(f32[2,224,64]{1,2,0:T(8,128)S(1)} %broadcast_multiply_fusion) | copy-start | bytes 344068
  617.4 4.9 copy-start.5
Sparse Core Ops, SparseCore 0:
  248.5 259.1 all-reduce.2
  541.9 71.3 all-reduce.4

commit v2 on v0

--- a/solution.py
+++ b/solution.py
@@ -43,7 +43,7 @@
     delta = gradient + feedback[0]
     left_part = jnp.einsum("kfd,kfr->kdr", delta, right_factor, precision=highest)
     replicas = lax.axis_size("rep")
-    left_mean = lax.psum(left_part, ("fsdp", "rep")) / replicas
+    left_mean = lax.psum(lax.psum(left_part, "rep"), "fsdp") / replicas
     basis = solve_basis(left_mean, local_gram(left_mean))
     right_part = jnp.einsum("kfd,kdr->kfr", delta, basis, precision=highest)
     right_next = lax.psum(right_part, "rep") / replicas

time: 521 us -> 456 us (0.88)
  waiting for transfers between devices: 414 us -> 349 us
    psum x1 -> x2, waiting for transfers between devices: 258 us -> 192 us  [per_device(): left_mean = lax.psum(lax.psum(left_part, 'rep'), 'fsdp') / replicas]
  transfers between devices with their start and end apart: 3 -> 4, of which waited for: 3 -> 4; matrix products, arithmetic and copies ran while one was open for 0% -> 0% of each run, Pallas kernels for 0% -> 0%
where the time goes in v2:
time: 456 us
  waiting for transfers between devices  349 us (77%)
  matrix products  62.1 us (14%)
  other arithmetic  29.6 us (6%)
  between operations  13.9 us (3%)
    psum x2, waiting for transfers between devices, per_device(): left_mean = lax.psum(lax.psum(left_part, 'rep'), 'fsdp') / replicas  192 us
    all_gather x1, waiting for transfers between devices, per_device(): segment = lax.all_gather(own_rows, 'fsdp', axis=0, tiled=True)  83.1 us
    psum x1, waiting for transfers between devices, per_device(): right_next = lax.psum(right_part, 'rep') / replicas  73 us
    dot_general x1, matrix products, per_device(): term_gate = jnp.dot(grad_gate, segment, preferred_element_type=jnp.float32)  20.5 us
    dot_general x1, matrix products, per_device(): lax.dot_general(weight[0], segment, contract_last, preferred_element_type...  13 us
    another operation x4, other arithmetic, solve_basis(): lower_factor = jnp.linalg.cholesky(gram_matrix)  11.9 us
    another operation x3, other arithmetic, solve_basis(): lax.linalg.triangular_solve(lower_factor, factor, left_side=False, lower=...  9.92 us
    dot_general x1, matrix products, per_device(): term_up = jnp.dot(grad_up, segment, preferred_element_type=jnp.float32)  9.73 us
  transfers between devices with their start and end apart: 4, of which 4 were waited for; matrix products, arithmetic and copies ran while one was open for 0% of the time, Pallas kernels for 0%

profile of v2, /device:TPU:2, one launch (start us, length us, event | category | flops | bytes accessed | tf_op | source)
XLA Modules:
  0.0 456.1 jit_solution(18000397189045079013)
XLA Ops:
  7.2 0.0 copy-start
  7.2 0.0 all-gather.3.cloned.1.call-start
  7.2 0.7 all-gather.3.cloned.1.call-update
  7.9 0.0 all-reduce.4.cloned.1.call-start
  8.0 83.1 %all-gather.3.cloned.1.call-done = bf16[1,4096,2048]{2,1,0:T(8,128)(2,1)} async-done(((bf16[1,128,2048]{2,1,0:T(8,128)(2,1)}), bf16[1,4096,2048]{2,1,0:T(8,128)(2,1)}) %all-gather.3.cloned.1.call-update) | async-done | bytes 16777232 | tf_op jit(solution)/shard_map/all_gather | solution.py:31
  91.1 13.0 %fusion.4 = f32[224,4096]{1,0:T(8,128)} fusion(bf16[1,4096,2048]{2,1,0:T(8,128)(2,1)} %all-gather.3.cloned.1.call-done, bf16[2,224,2048]{2,1,0:T(8,128)(2,1)} %param.8), kind=kOutput, calls=%fused_computation.4 | convolution fusion | flops 3758096384 | bytes 21364736 | tf_op jit(solution)/shard_map/dot_general | solution.py:33
  104.1 20.5 %fusion.25 = f32[1,224,2048]{2,1,0:T(8,128)S(1)} fusion(bf16[1,4096,2048]{2,1,0:T(8,128)(2,1)} %all-gather.3.cloned.1.call-done, f32[224,4096]{1,0:T(8,128)} %fusion.4, bf16[1,224,4096]{2,1,0:T(8,128)(2,1)} %param.7, bf16[2,224,2048]{2,1,0:T(8,128)(2,1)} %param.8), kind=kOutput, calls=%fused_computation.21 | convolution fusion | flops 7526285312 | bytes 41811968 | tf_op jit(solution)/shard_map/dot_general | solution.py:40
  124.7 0.0 copy-start.1
  124.7 9.7 %fusion.30 = f32[1,224,2048]{2,1,0:T(8,128)S(1)} fusion(bf16[1,4096,2048]{2,1,0:T(8,128)(2,1)} %all-gather.3.cloned.1.call-done, f32[224,4096]{1,0:T(8,128)} %fusion.4, bf16[1,224,4096]{2,1,0:T(8,128)(2,1)} %param.7), kind=kOutput, calls=%fused_computation.22 | convolution fusion | flops 3764518912 | bytes 24117248 | tf_op jit(solution)/shard_map/dot_general | solution.py:41
  134.4 0.0 copy-start.3
  134.4 1.2 copy-done.3
  135.7 0.0 copy-done
  135.7 0.0 copy-done.1
  135.7 3.6 fusion.57
  139.3 0.0 all-reduce.4.cloned.1.call-update
  139.3 0.0 all-reduce.6.cloned.1.call-start
  139.3 75.7 %all-reduce.4.cloned.1.call-done = f32[2,2048,64]{1,2,0:T(8,128)} async-done(((f32[2,2048,64]{1,2,0:T(8,128)}), f32[2,2048,64]{1,2,0:T(8,128)}) %all-reduce.4.cloned.1.call-update) | async-done | bytes 1048592 | tf_op jit(solution)/shard_map/psum | solution.py:46
  215.0 0.0 all-reduce.6.cloned.1.call-update
  215.0 0.2 all-reduce.8.cloned.1.call-start
  215.3 116.2 %all-reduce.6.cloned.1.call-done = f32[2,2048,64]{1,2,0:T(8,128)} async-done(((f32[2,2048,64]{1,2,0:T(8,128)}), f32[2,2048,64]{1,2,0:T(8,128)}) %all-reduce.6.cloned.1.call-update) | async-done | bytes 1048592 | tf_op jit(solution)/shard_map/psum | solution.py:46
  331.5 2.7 fusion.40
  334.2 0.1 copy.12
  334.3 11.7 %custom-call.7 = f32[2,64,64]{2,1,0:T(8,128)S(1)} custom-call(f32[2,64,64]{2,1,0:T(8,128)S(1)} %fusion.51), custom_call_target="Cholesky" | custom-call | tf_op jit(solution)/shard_map/jit(cholesky)/cholesky | solution.py:17
  346.1 0.1 compare_reduce_fusion
  346.2 0.1 select_bitcast_fusion
  346.3 9.8 %custom-call.8 = f32[2,1,64,64]{2,3,1,0:T(8,128)S(1)} custom-call(f32[2,1,64,64]{3,2,1,0:T(8,128)S(1)} %select_bitcast_fusion), custom_call_target="InvertDiagBlocksLowerTriangular" | custom-call | tf_op jit(solution)/shard_map/triangular_solve | solution.py:18
  356.1 2.3 fusion.38
  358.5 7.1 %fusion.56 = f32[2,224,64]{1,2,0:T(8,128)} fusion(f32[2,2048,64]{1,2,0:T(8,128)S(1)} %fusion.38, f32[1,224,2048]{2,1,0:T(8,128)} %copy-done.3, f32[1,224,2048]{2,1,0:T(8,128)S(1)} %fusion.25, f32[1,2,224,2048]{3,2,1,0:T(8,128)} %param.9), kind=kOutput, calls=%fused_computation.52 | convolution fusion | flops 706478080 | bytes 8503296 | tf_op jit(solution)/shard_map/kfd,kdr->kfr/dot_general | solution.py:48
  365.6 0.0 all-reduce.8.cloned.1.call-update
  365.6 73.0 %all-reduce.8.cloned.1.call-done = f32[2,224,64]{1,2,0:T(8,128)} async-done(((f32[2,224,64]{1,2,0:T(8,128)}), f32[2,224,64]{1,2,0:T(8,128)}) %all-reduce.8.cloned.1.call-update) | async-done | bytes 114704 | tf_op jit(solution)/shard_map/psum | solution.py:49
  438.6 0.0 copy-start.2
  438.6 1.1 broadcast_multiply_fusion
  439.7 0.0 copy-start.4
  439.7 3.1 fusion.58
  442.8 0.0 copy-done.2
  442.8 0.0 copy-start.5
  442.8 4.8 %subtract_bitcast_fusion = f32[1,2,224,2048]{3,2,1,0:T(8,128)} fusion(f32[2,224,2048]{2,1,0:T(8,128)S(1)} %fusion.58, f32[1,2,224,2048]{3,2,1,0:T(8,128)S(1)} %copy-done.2, f32[1,224,2048]{2,1,0:T(8,128)} %copy-done.3, f32[1,224,2048]{2,1,0:T(8,128)S(1)} %fusion.25), kind=kLoop, calls=%fused_computation.15 | loop fusion | flops 2752512 | bytes 14680064 | tf_op jit(solution)/shard_map/broadcast_in_dim | solution.py:51
  447.6 0.0 copy-done.4
  447.6 0.0 copy-done.5
  447.7 1.9 subtract_convert_fusion
  (4 shorter events, 0.1 us)
Async XLA Ops:
  7.2 128.5 %copy-start = (f32[2,224,64]{1,2,0:T(8,128)S(1)}, f32[2,224,64]{1,2,0:T(8,128)}, u32[]{:S(2)}) copy-start(f32[2,224,64]{1,2,0:T(8,128)} %param.11) | copy-start | bytes 344068
  7.2 83.9 %all-gather.3.cloned.1.call-start = ((), (), s32[]{:S(2)}) async-start(), calls=%async_computation.3 | async-start | bytes 17301504 | tf_op jit(solution)/shard_map/all_gather | solution.py:31
  7.9 207.1 %all-reduce.4.cloned.1.call-start = ((), (), s32[]{:S(2)}) async-start(), calls=%async_computation | async-start | bytes 2097152 | tf_op jit(solution)/shard_map/psum | solution.py:46
  124.7 11.0 %copy-start.1 = (f32[1,2,224,2048]{3,2,1,0:T(8,128)S(1)}, f32[1,2,224,2048]{3,2,1,0:T(8,128)}, u32[]{:S(2)}) copy-start(f32[1,2,224,2048]{3,2,1,0:T(8,128)} %param.9) | copy-start | bytes 11010052
  134.4 1.3 copy-start.3
  139.3 192.3 %all-reduce.6.cloned.1.call-start = ((), (), s32[]{:S(2)}) async-start(), calls=%async_computation.1 | async-start | bytes 2097152 | tf_op jit(solution)/shard_map/psum | solution.py:46
  215.0 223.6 %all-reduce.8.cloned.1.call-start = ((), (), s32[]{:S(2)}) async-start(), calls=%async_computation.2 | async-start | bytes 262144 | tf_op jit(solution)/shard_map/psum | solution.py:49
  438.6 4.2 copy-start.2
  439.7 8.0 %copy-start.4 = (f32[2,224,64]{1,2,0:T(8,128)}, f32[2,224,64]{1,2,0:T(8,128)S(1)}, u32[]{:S(2)}) copy-start(f32[2,224,64]{1,2,0:T(8,128)S(1)} %broadcast_multiply_fusion) | copy-start | bytes 344068
  442.8 4.9 %copy-start.5 = (f32[2,224,256]{2,1,0:T(8,128)S(1)}, f32[2,224,256]{2,1,0:T(8,128)}, u32[]{:S(2)}) copy-start(f32[2,224,256]{2,1,0:T(8,128)} %param.10) | copy-start | bytes 1376260
Sparse Core Ops, SparseCore 0:
  10.5 80.4 all-gather.2
  139.4 75.5 all-reduce.3
  218.2 113.2 all-reduce.5
  365.7 72.8 all-reduce.7
